TPU v7x, 128 devices: a whole 4x4x4 slice. The times are simulated.
128 devices in a mesh: dp: 8 (over z_hi, x), ctx: 16 (over z_lo, y, core).
Axes of the slice: x: 4, y: 4, z: 4 (z_hi: 2, z_lo: 2; z = z_hi * 2 + z_lo), core: 2. Of those that a mesh axis runs over, the one named last changes fastest.
Arguments:
- resid: bfloat16 [16384, 4096], P(('dp', 'ctx')), may hold values from -6 to 6
- query: bfloat16 [16384, 2048], P(('dp', 'ctx')), may hold values from -40 to 40
- keys: bfloat16 [16384, 512], P(('dp', 'ctx')), may hold values from -40 to 40
- values: bfloat16 [16384, 512], P(('dp', 'ctx')), may hold values from -6 to 6
- doc_lengths: int32 [16], replicated, may hold values from 1 to 2048, 16384 in all
- w_out: bfloat16 [2048, 4096], P('dp'), may hold values from -0.125 to 0.125
- norm_gain: float32 [4096], replicated, may hold values from 0.1 to 1.9
- w_gate: bfloat16 [4096, 7168], P(None, 'dp'), may hold values from -0.09375 to 0.09375
- w_up: bfloat16 [4096, 7168], P(None, 'dp'), may hold values from -0.09375 to 0.09375
- w_down: bfloat16 [7168, 4096], P('dp'), may hold values from -0.0625 to 0.0625
Outputs:
- layer_out: bfloat16 [16384, 4096], P(('dp', 'ctx'))
Inputs may be any that keep to these rules, and one draw needn't show every extreme that they name: `doc_lengths`: the lengths sum to 16384, and the longest is exactly 2048.
All inputs are finite; a program needn't handle non-finite values.
Results may differ from a plain program's by a relative error of at most 0.015.
Values may be sent and summed in bfloat16 or wider, within the bound.
A program may use at most 192 MiB of HBM per device.

v0:
```python
import math

import jax
import jax.numpy as jnp
from jax import lax
from jax.sharding import PartitionSpec as P

HEAD_DIM = 128


ROPE_BASE = 500000.0
EPS = 1e-05
NEG_FILL = -1e30


def from_behind(block, axis, distance):
    devices = range(lax.axis_size(axis))
    route = [(i - distance, i) for i in devices if i - distance in devices]
    return lax.ppermute(block, axis, route)


def rope_tables(rel_pos, head_dim):
    half_dim = head_dim // 2
    freq_index = jnp.arange(half_dim, dtype=jnp.float32)
    inv_freq = jnp.exp(freq_index * (-2.0 * math.log(ROPE_BASE) / head_dim))
    angles = rel_pos.astype(jnp.float32)[:, None] * inv_freq[None, :]
    return (jnp.cos(angles), jnp.sin(angles))


def rotate(field, cosine, sine_val, num_heads, head_dim):
    row_count = field.shape[0]
    half_dim = head_dim // 2
    shaped = field.astype(jnp.float32).reshape(row_count, num_heads, head_dim)
    first_half = shaped[..., :half_dim]
    second_half = shaped[..., half_dim:]
    cos_b = cosine[:, None, :]
    sin_b = sine_val[:, None, :]
    turned = jnp.concatenate(
        [first_half * cos_b - second_half * sin_b, second_half * cos_b + first_half * sin_b],
        axis=-1,
    )
    return turned.reshape(row_count, num_heads * head_dim).astype(jnp.bfloat16)


def doc_starts(doc_lengths, positions):
    doc_ends = jnp.cumsum(doc_lengths)
    starts = doc_ends - doc_lengths
    inside = starts[None, :] <= positions[:, None]
    return jnp.max(jnp.where(inside, starts[None, :], 0), axis=1)


def online_update(
    softmax_state, q_group, key_rows, value_rows, key_pos, query_pos, query_start, score_scale
):
    row_max, row_sum, weighted = softmax_state
    kv_heads = q_group.shape[0]
    head_dim = q_group.shape[2]
    key_heads = key_rows.reshape(key_rows.shape[0], kv_heads, head_dim).transpose(1, 0, 2)
    value_heads = value_rows.reshape(value_rows.shape[0], kv_heads, head_dim).transpose(1, 0, 2)
    scores = (
        jnp.einsum("aqd,akd->aqk", q_group, key_heads, preferred_element_type=jnp.float32)
        * score_scale
    )
    allowed = (key_pos[None, :] >= query_start[:, None]) & (key_pos[None, :] <= query_pos[:, None])
    group_size = q_group.shape[1] // query_pos.shape[0]
    allowed = jnp.tile(allowed, (group_size, 1))[None]
    scores = jnp.where(allowed, scores, NEG_FILL)
    new_max = jnp.maximum(row_max, jnp.max(scores, axis=-1))
    weights = jnp.where(allowed, jnp.exp(scores - new_max[..., None]), 0.0)
    factor = jnp.exp(row_max - new_max)
    row_sum = row_sum * factor + jnp.sum(weights, axis=-1)
    weighted = weighted * factor[..., None] + jnp.einsum(
        "aqk,akd->aqd",
        weights.astype(jnp.bfloat16),
        value_heads,
        preferred_element_type=jnp.float32,
    )
    return (new_max, row_sum, weighted)


def per_device(resid, query, keys, values, doc_lengths, w_out, norm_gain, w_gate, w_up, w_down):
    tok_rows = resid.shape[0]
    dp_count = lax.axis_size("dp")
    ctx_count = lax.axis_size("ctx")
    reach_devs = min(16, dp_count * ctx_count // 4)
    head_dim = HEAD_DIM
    kv_heads = keys.shape[1] // head_dim
    num_heads = query.shape[1] // head_dim
    group_size = num_heads // kv_heads
    my_block = lax.axis_index(("dp", "ctx"))
    local_index = jnp.arange(tok_rows, dtype=jnp.int32)
    query_pos = my_block * tok_rows + local_index
    query_start = doc_starts(doc_lengths, query_pos)
    cosine, sine_val = rope_tables(query_pos - query_start, head_dim)
    q_rot = rotate(query, cosine, sine_val, num_heads, head_dim)
    k_rot = rotate(keys, cosine, sine_val, kv_heads, head_dim)
    q_group = (
        q_rot.reshape(tok_rows, kv_heads, group_size, head_dim)
        .transpose(1, 2, 0, 3)
        .reshape(kv_heads, group_size * tok_rows, head_dim)
    )
    score_scale = 1.0 / math.sqrt(head_dim)
    softmax_state = (
        jnp.full((kv_heads, group_size * tok_rows), NEG_FILL, jnp.float32),
        jnp.zeros((kv_heads, group_size * tok_rows), jnp.float32),
        jnp.zeros((kv_heads, group_size * tok_rows, head_dim), jnp.float32),
    )
    kv_pair = jnp.stack([k_rot, values])
    softmax_state = online_update(
        softmax_state, q_group, k_rot, values, query_pos, query_pos, query_start, score_scale
    )

    def cycle_free_step(turn_index, loop_state):
        inner_state, moving = loop_state
        moving = from_behind(moving, ("dp", "ctx"), 1)
        source = my_block - turn_index - 1
        inner_state = online_update(
            inner_state,
            q_group,
            moving[0],
            moving[1],
            source * tok_rows + local_index,
            query_pos,
            query_start,
            score_scale,
        )
        return (inner_state, moving)

    softmax_state, _ = lax.fori_loop(0, reach_devs, cycle_free_step, (softmax_state, kv_pair))
    row_max, row_sum, weighted = softmax_state
    heads_out = (weighted / row_sum[..., None]).reshape(kv_heads, group_size, tok_rows, head_dim)
    heads_out = (
        heads_out.transpose(2, 0, 1, 3).reshape(tok_rows, num_heads * head_dim).astype(jnp.bfloat16)
    )
    spread = lax.all_to_all(heads_out, "dp", split_axis=1, concat_axis=0, tiled=True)
    projected = lax.psum_scatter(
        jnp.dot(spread, w_out, preferred_element_type=jnp.float32).astype(jnp.bfloat16),
        "dp",
        scatter_dimension=0,
        tiled=True,
    ).astype(jnp.float32)
    residual_sum = resid.astype(jnp.float32) + projected
    mean_sq = jnp.mean(residual_sum * residual_sum, axis=1, keepdims=True)
    normed = (residual_sum * lax.rsqrt(mean_sq + EPS) * norm_gain).astype(jnp.bfloat16)
    piece_rows = lax.all_gather(normed, "dp", axis=0, tiled=True)
    gate_val = jnp.dot(piece_rows, w_gate, preferred_element_type=jnp.float32)
    up_val = jnp.dot(piece_rows, w_up, preferred_element_type=jnp.float32)
    hidden_act = (jax.nn.silu(gate_val) * up_val).astype(jnp.bfloat16)
    partial_rows = jnp.dot(hidden_act, w_down, preferred_element_type=jnp.float32)
    mlp_out = lax.psum_scatter(
        partial_rows.astype(jnp.bfloat16), "dp", scatter_dimension=0, tiled=True
    ).astype(jnp.float32)
    return (residual_sum + mlp_out).astype(jnp.bfloat16)


def solution(mesh):
    return jax.shard_map(
        per_device,
        mesh=mesh,
        in_specs=(
            P(("dp", "ctx"), None),
            P(("dp", "ctx"), None),
            P(("dp", "ctx"), None),
            P(("dp", "ctx"), None),
            P(),
            P("dp", None),
            P(),
            P(None, "dp"),
            P(None, "dp"),
            P("dp", None),
        ),
        out_specs=P(("dp", "ctx"), None),
        check_vma=False,
    )
```

profile of v0, /device:TPU:0, one launch (start us, length us, event | category | flops | bytes accessed | tf_op | source)
XLA Modules:
  0.0 747.6 jit_solution(9612714527674316773)
XLA Ops:
  16.7 250.3 %while.22 = (s32[]{:T(128)}, f32[4,512]{1,0:T(4,128)S(1)}, f32[4,512]{1,0:T(4,128)S(1)}, f32[4,512,128]{2,1,0:T(8,128)S(1)}, bf16[2,128,512]{1,2,0:T(8,128)(2,1)...) while((s32[]{:T(128)}, f32[4,512]{1,0:T(4,128)S(1)}, ...), condition=%wide.region_7.8_spmd.clone, body=%wide.region_4.7_spmd.clone.sunk | while | flops 137154816 | bytes 9210569 | solution.py:129
  27.3 6.6 collective-permute-start
  43.3 6.5 collective-permute-start
  59.2 6.5 collective-permute-start
  75.2 6.5 collective-permute-start
  91.1 6.5 collective-permute-start
  107.0 6.5 collective-permute-start
  123.0 6.5 collective-permute-start
  138.9 6.5 collective-permute-start
  154.8 6.5 collective-permute-start
  170.8 6.5 collective-permute-start
  186.7 6.5 collective-permute-start
  202.6 6.5 collective-permute-start
  218.6 6.5 collective-permute-start
  234.5 6.5 collective-permute-start
  250.4 7.2 collective-permute-start
  269.4 87.4 %all_to_all.16 = bf16[128,8,256]{0,2,1:T(8,128)(2,1)S(1)} all-to-all(bf16[128,8,256]{0,2,1:T(8,128)(2,1)S(1)} %bitcast.89), channel_id=1, replica_groups=mesh['dp'=8,'ctx'=16] {'dp'}, dimensions={1} | all-to-all | bytes 1048576 | tf_op jit(solution)/shard_map/all_to_all | solution.py:135
  357.0 5.6 convolution_convert_fusion.1
  362.7 110.1 %reduce-scatter.3.cloned.1.call-done = bf16[128,4096]{1,0:T(8,128)(2,1)} async-done(((bf16[1024,4096]{1,0:T(8,128)(2,1)}), bf16[128,4096]{1,0:T(8,128)(2,1)}) %reduce-scatter.3.cloned.1.call-update) | async-done | bytes 1048592 | tf_op jit(solution)/shard_map/reduce_scatter | solution.py:136
  477.3 106.6 %all-gather.2.cloned.1.call-done = bf16[1024,4096]{1,0:T(8,128)(2,1)} async-done(((bf16[128,4096]{1,0:T(8,128)(2,1)}), bf16[1024,4096]{1,0:T(8,128)(2,1)}) %all-gather.2.cloned.1.call-update) | async-done | bytes 8388624 | tf_op jit(solution)/shard_map/all_gather | solution.py:145
  583.9 14.6 %fusion.31 = f32[1024,896]{1,0:T(8,128)} fusion(bf16[1024,4096]{1,0:T(8,128)(2,1)} %all-gather.2.cloned.1.call-done, bf16[4096,896]{1,0:T(8,128)(2,1)} %param.19), kind=kOutput, calls=%fused_computation.67 | convolution fusion | flops 7516192768 | bytes 19398656 | tf_op jit(solution)/shard_map/dot_general | solution.py:146
  598.5 26.7 %convolution_convert_fusion = bf16[1024,4096]{1,0:T(8,128)(2,1)} fusion(bf16[896,4096]{1,0:T(8,128)(2,1)} %param.21, f32[1024,896]{1,0:T(8,128)} %fusion.31, bf16[1024,4096]{1,0:T(8,128)(2,1)} %all-gather.2.cloned.1.call-done, bf16[4096,896]{1,0:T(8,128)(2,1)} %param.20), kind=kOutput, calls=%fused_computation.20 | convolution fusion | flops 15042084864 | bytes 35127296 | tf_op jit(solution)/shard_map/dot_general | solution.py:149
  625.2 112.8 %reduce-scatter.5.cloned.1.call-done = bf16[128,4096]{1,0:T(8,128)(2,1)} async-done(((bf16[1024,4096]{1,0:T(8,128)(2,1)}), bf16[128,4096]{1,0:T(8,128)(2,1)}) %reduce-scatter.5.cloned.1.call-update) | async-done | bytes 1048592 | tf_op jit(solution)/shard_map/reduce_scatter | solution.py:150
  738.1 3.0 add_convert_fusion
  (314 shorter events, 167.4 us)
Async XLA Ops:
  6.5 350.5 %copy-start = (bf16[256,4096]{1,0:T(8,128)(2,1)S(1)}, bf16[256,4096]{1,0:T(8,128)(2,1)}, u32[]{:S(2)}) copy-start(bf16[256,4096]{1,0:T(8,128)(2,1)} %param.17) | copy-start | bytes 6291460
  6.5 466.3 %reduce-scatter.3.cloned.1.call-start = ((), (), s32[]{:S(2)}) async-start(), calls=%async_computation.3 | async-start | bytes 9437184 | tf_op jit(solution)/shard_map/reduce_scatter | solution.py:136
  14.1 1.8 copy-start.5
  16.7 2.6 collective-permute-start
  27.3 7.9 %collective-permute-start = (bf16[2,128,512]{1,2,0:T(8,128)(2,1)}, bf16[2,128,512]{1,2,0:T(8,128)(2,1)S(1)}, u32[]{:S(2)}, u32[]{:S(2)}) collective-permute-start(bf16[2,128,512]{1,2,0:T(8,128)(2,1)} %get-tuple-element.391), channel_id=1, source_target_pairs={{0,1},{1,2},{2,3},{3,4},{4,5},{5,6},{6,7},{7,8},{8,9},{9,10},{10,1... | collective-permute-start | bytes 786440 | tf_op jit(solution)/shard_map/while/body/eval_jaxpr/ppermute | solution.py:19
  43.3 7.9 %collective-permute-start = (bf16[2,128,512]{1,2,0:T(8,128)(2,1)}, bf16[2,128,512]{1,2,0:T(8,128)(2,1)S(1)}, u32[]{:S(2)}, u32[]{:S(2)}) collective-permute-start(bf16[2,128,512]{1,2,0:T(8,128)(2,1)} %get-tuple-element.391), channel_id=1, source_target_pairs={{0,1},{1,2},{2,3},{3,4},{4,5},{5,6},{6,7},{7,8},{8,9},{9,10},{10,1... | collective-permute-start | bytes 786440 | tf_op jit(solution)/shard_map/while/body/eval_jaxpr/ppermute | solution.py:19
  59.2 7.9 %collective-permute-start = (bf16[2,128,512]{1,2,0:T(8,128)(2,1)}, bf16[2,128,512]{1,2,0:T(8,128)(2,1)S(1)}, u32[]{:S(2)}, u32[]{:S(2)}) collective-permute-start(bf16[2,128,512]{1,2,0:T(8,128)(2,1)} %get-tuple-element.391), channel_id=1, source_target_pairs={{0,1},{1,2},{2,3},{3,4},{4,5},{5,6},{6,7},{7,8},{8,9},{9,10},{10,1... | collective-permute-start | bytes 786440 | tf_op jit(solution)/shard_map/while/body/eval_jaxpr/ppermute | solution.py:19
  75.2 7.9 %collective-permute-start = (bf16[2,128,512]{1,2,0:T(8,128)(2,1)}, bf16[2,128,512]{1,2,0:T(8,128)(2,1)S(1)}, u32[]{:S(2)}, u32[]{:S(2)}) collective-permute-start(bf16[2,128,512]{1,2,0:T(8,128)(2,1)} %get-tuple-element.391), channel_id=1, source_target_pairs={{0,1},{1,2},{2,3},{3,4},{4,5},{5,6},{6,7},{7,8},{8,9},{9,10},{10,1... | collective-permute-start | bytes 786440 | tf_op jit(solution)/shard_map/while/body/eval_jaxpr/ppermute | solution.py:19
  91.1 7.9 %collective-permute-start = (bf16[2,128,512]{1,2,0:T(8,128)(2,1)}, bf16[2,128,512]{1,2,0:T(8,128)(2,1)S(1)}, u32[]{:S(2)}, u32[]{:S(2)}) collective-permute-start(bf16[2,128,512]{1,2,0:T(8,128)(2,1)} %get-tuple-element.391), channel_id=1, source_target_pairs={{0,1},{1,2},{2,3},{3,4},{4,5},{5,6},{6,7},{7,8},{8,9},{9,10},{10,1... | collective-permute-start | bytes 786440 | tf_op jit(solution)/shard_map/while/body/eval_jaxpr/ppermute | solution.py:19
  107.0 7.9 %collective-permute-start = (bf16[2,128,512]{1,2,0:T(8,128)(2,1)}, bf16[2,128,512]{1,2,0:T(8,128)(2,1)S(1)}, u32[]{:S(2)}, u32[]{:S(2)}) collective-permute-start(bf16[2,128,512]{1,2,0:T(8,128)(2,1)} %get-tuple-element.391), channel_id=1, source_target_pairs={{0,1},{1,2},{2,3},{3,4},{4,5},{5,6},{6,7},{7,8},{8,9},{9,10},{10,1... | collective-permute-start | bytes 786440 | tf_op jit(solution)/shard_map/while/body/eval_jaxpr/ppermute | solution.py:19
  123.0 7.9 %collective-permute-start = (bf16[2,128,512]{1,2,0:T(8,128)(2,1)}, bf16[2,128,512]{1,2,0:T(8,128)(2,1)S(1)}, u32[]{:S(2)}, u32[]{:S(2)}) collective-permute-start(bf16[2,128,512]{1,2,0:T(8,128)(2,1)} %get-tuple-element.391), channel_id=1, source_target_pairs={{0,1},{1,2},{2,3},{3,4},{4,5},{5,6},{6,7},{7,8},{8,9},{9,10},{10,1... | collective-permute-start | bytes 786440 | tf_op jit(solution)/shard_map/while/body/eval_jaxpr/ppermute | solution.py:19
  138.9 7.9 %collective-permute-start = (bf16[2,128,512]{1,2,0:T(8,128)(2,1)}, bf16[2,128,512]{1,2,0:T(8,128)(2,1)S(1)}, u32[]{:S(2)}, u32[]{:S(2)}) collective-permute-start(bf16[2,128,512]{1,2,0:T(8,128)(2,1)} %get-tuple-element.391), channel_id=1, source_target_pairs={{0,1},{1,2},{2,3},{3,4},{4,5},{5,6},{6,7},{7,8},{8,9},{9,10},{10,1... | collective-permute-start | bytes 786440 | tf_op jit(solution)/shard_map/while/body/eval_jaxpr/ppermute | solution.py:19
  154.8 7.9 %collective-permute-start = (bf16[2,128,512]{1,2,0:T(8,128)(2,1)}, bf16[2,128,512]{1,2,0:T(8,128)(2,1)S(1)}, u32[]{:S(2)}, u32[]{:S(2)}) collective-permute-start(bf16[2,128,512]{1,2,0:T(8,128)(2,1)} %get-tuple-element.391), channel_id=1, source_target_pairs={{0,1},{1,2},{2,3},{3,4},{4,5},{5,6},{6,7},{7,8},{8,9},{9,10},{10,1... | collective-permute-start | bytes 786440 | tf_op jit(solution)/shard_map/while/body/eval_jaxpr/ppermute | solution.py:19
  170.8 7.9 %collective-permute-start = (bf16[2,128,512]{1,2,0:T(8,128)(2,1)}, bf16[2,128,512]{1,2,0:T(8,128)(2,1)S(1)}, u32[]{:S(2)}, u32[]{:S(2)}) collective-permute-start(bf16[2,128,512]{1,2,0:T(8,128)(2,1)} %get-tuple-element.391), channel_id=1, source_target_pairs={{0,1},{1,2},{2,3},{3,4},{4,5},{5,6},{6,7},{7,8},{8,9},{9,10},{10,1... | collective-permute-start | bytes 786440 | tf_op jit(solution)/shard_map/while/body/eval_jaxpr/ppermute | solution.py:19
  186.7 7.9 %collective-permute-start = (bf16[2,128,512]{1,2,0:T(8,128)(2,1)}, bf16[2,128,512]{1,2,0:T(8,128)(2,1)S(1)}, u32[]{:S(2)}, u32[]{:S(2)}) collective-permute-start(bf16[2,128,512]{1,2,0:T(8,128)(2,1)} %get-tuple-element.391), channel_id=1, source_target_pairs={{0,1},{1,2},{2,3},{3,4},{4,5},{5,6},{6,7},{7,8},{8,9},{9,10},{10,1... | collective-permute-start | bytes 786440 | tf_op jit(solution)/shard_map/while/body/eval_jaxpr/ppermute | solution.py:19
  202.6 7.9 %collective-permute-start = (bf16[2,128,512]{1,2,0:T(8,128)(2,1)}, bf16[2,128,512]{1,2,0:T(8,128)(2,1)S(1)}, u32[]{:S(2)}, u32[]{:S(2)}) collective-permute-start(bf16[2,128,512]{1,2,0:T(8,128)(2,1)} %get-tuple-element.391), channel_id=1, source_target_pairs={{0,1},{1,2},{2,3},{3,4},{4,5},{5,6},{6,7},{7,8},{8,9},{9,10},{10,1... | collective-permute-start | bytes 786440 | tf_op jit(solution)/shard_map/while/body/eval_jaxpr/ppermute | solution.py:19
  218.6 7.9 %collective-permute-start = (bf16[2,128,512]{1,2,0:T(8,128)(2,1)}, bf16[2,128,512]{1,2,0:T(8,128)(2,1)S(1)}, u32[]{:S(2)}, u32[]{:S(2)}) collective-permute-start(bf16[2,128,512]{1,2,0:T(8,128)(2,1)} %get-tuple-element.391), channel_id=1, source_target_pairs={{0,1},{1,2},{2,3},{3,4},{4,5},{5,6},{6,7},{7,8},{8,9},{9,10},{10,1... | collective-permute-start | bytes 786440 | tf_op jit(solution)/shard_map/while/body/eval_jaxpr/ppermute | solution.py:19
  234.5 7.9 %collective-permute-start = (bf16[2,128,512]{1,2,0:T(8,128)(2,1)}, bf16[2,128,512]{1,2,0:T(8,128)(2,1)S(1)}, u32[]{:S(2)}, u32[]{:S(2)}) collective-permute-start(bf16[2,128,512]{1,2,0:T(8,128)(2,1)} %get-tuple-element.391), channel_id=1, source_target_pairs={{0,1},{1,2},{2,3},{3,4},{4,5},{5,6},{6,7},{7,8},{8,9},{9,10},{10,1... | collective-permute-start | bytes 786440 | tf_op jit(solution)/shard_map/while/body/eval_jaxpr/ppermute | solution.py:19
  250.4 8.5 %collective-permute-start = (bf16[2,128,512]{1,2,0:T(8,128)(2,1)}, bf16[2,128,512]{1,2,0:T(8,128)(2,1)S(1)}, u32[]{:S(2)}, u32[]{:S(2)}) collective-permute-start(bf16[2,128,512]{1,2,0:T(8,128)(2,1)} %get-tuple-element.391), channel_id=1, source_target_pairs={{0,1},{1,2},{2,3},{3,4},{4,5},{5,6},{6,7},{7,8},{8,9},{9,10},{10,1... | collective-permute-start | bytes 786440 | tf_op jit(solution)/shard_map/while/body/eval_jaxpr/ppermute | solution.py:19
  362.6 110.2 %copy-start.3 = (bf16[128,4096]{1,0:T(8,128)(2,1)S(1)}, bf16[128,4096]{1,0:T(8,128)(2,1)}, u32[]{:S(2)}) copy-start(bf16[128,4096]{1,0:T(8,128)(2,1)} %param.12) | copy-start | bytes 3145732
  362.6 111.9 %copy-start.6 = (f32[4096]{0:T(1024)S(1)}, f32[4096]{0:T(1024)}, u32[]{:S(2)}) copy-start(f32[4096]{0:T(1024)} %param.18) | copy-start | bytes 49156
  362.6 221.3 %all-gather.2.cloned.1.call-start = ((), (), s32[]{:S(2)}) async-start(), calls=%async_computation.4 | async-start | bytes 9437184 | tf_op jit(solution)/shard_map/all_gather | solution.py:145
  477.1 261.0 %reduce-scatter.5.cloned.1.call-start = ((), (), s32[]{:S(2)}) async-start(), calls=%async_computation.5 | async-start | bytes 9437184 | tf_op jit(solution)/shard_map/reduce_scatter | solution.py:150
  625.2 115.8 %copy-start.1 = (bf16[256,4096]{1,0:T(8,128)(2,1)S(1)}, bf16[256,4096]{1,0:T(8,128)(2,1)}, u32[]{:S(2)}) copy-start(bf16[256,4096]{1,0:T(8,128)(2,1)} %param.17) | copy-start | bytes 6291460
  (2 other events, 2.6 us)
Sparse Core Ops, SparseCore 0:
  362.7 110.0 reduce-scatter.2
  477.2 106.6 all-gather.1
  625.3 112.6 reduce-scatter.4
where the time goes:
time: 750 us; the launch traced here: 748 us
  waiting for transfers between devices  347 us (46%)
  starting transfers between devices  100 us (13%)
  matrix products  96.2 us (13%)
  blocking collectives  87.4 us (12%)
  local copies, waits for them, and re-layouts  83.5 us (11%)
  other arithmetic  18.2 us (2%)
  between operations  13.3 us (2%)
    reduce_scatter x1, waiting for transfers between devices, per_device(): lax.psum_scatter(partial_rows.astype(jnp.bfloat16), 'dp', scatter_dimensi...  113 us
    reduce_scatter x1, waiting for transfers between devices, per_device(): lax.psum_scatter(jnp.dot(spread, w_out, preferred_element_type=jnp.float3...  110 us
    all_gather x1, waiting for transfers between devices, per_device(): piece_rows = lax.all_gather(normed, 'dp', axis=0, tiled=True)  107 us
    ppermute x16, starting transfers between devices, from_behind(): return lax.ppermute(block, axis, route)  100 us
    all_to_all x1, blocking collectives, per_device(): lax.all_to_all(heads_out, 'dp', split_axis=1, concat_axis=0, tiled=True)  87.4 us
    dot_general x1, matrix products, per_device(): jnp.dot(hidden_act, w_down, preferred_element_type=jnp.float32)  26.7 us
    squeeze x16, local copies, waits for them, and re-layouts, online_update(): value_rows.reshape(value_rows.shape[0], kv_heads, head_dim)  26.7 us
    dot_general x17, matrix products, online_update(): jnp.einsum('aqk,akd->aqd', weights.astype(jnp.bfloat16), value_heads, pre...  26.6 us
  transfers between devices with their start and end apart: 19, of which 19 were waited for; matrix products, arithmetic and copies ran while one was open for 0% of the time, Pallas kernels for 0%

commit v1 on v0

--- a/solution.py
+++ b/solution.py
@@ -3,6 +3,8 @@
 import jax
 import jax.numpy as jnp
 from jax import lax
+from jax.experimental import pallas as pl
+from jax.experimental.pallas import tpu as pltpu
 from jax.sharding import PartitionSpec as P
 
 HEAD_DIM = 128
@@ -76,6 +78,276 @@
         preferred_element_type=jnp.float32,
     )
     return (new_max, row_sum, weighted)
+
+
+MESH = pl.DeviceIdType.MESH
+
+
+def dp_neighbours():
+    dp_at = lax.axis_index("dp")
+    ctx_at = lax.axis_index("ctx")
+    ring = (dp_at // 4) * 4
+    x_at = dp_at % 4
+    right = (ring + (x_at + 1) % 4, ctx_at)
+    left = (ring + (x_at + 3) % 4, ctx_at)
+    across = ((dp_at + 4) % 8, ctx_at)
+    return right, left, across
+
+
+BLOCKS = ((0, 0), (1, 0), (0, 1), (0, 3), (0, 2), (1, 1), (1, 2), (1, 3))
+SLOT = {name: at for at, name in enumerate(BLOCKS)}
+
+
+def mlp_kernel(
+    normed_ref, resid_ref, gate_hbm, up_hbm, down_hbm, out_ref,
+    tokens, gate_w, up_w, down_w, hidden, sums,
+    far_1, far_2, near_1, near_2, cross_1, cross_2,
+    local_sem, send_sem, recv_sem,
+):
+    right, left, across = dp_neighbours()
+    rows = tokens.shape[1]
+    q = rows // 4
+    low, high = pl.ds(0, 2 * q), pl.ds(2 * q, 2 * q)
+    part = [pl.ds(i * q, q) for i in range(4)]
+
+    own = pltpu.make_async_copy(normed_ref, tokens.at[0], local_sem.at[0])
+    own.start()
+    loads = [
+        pltpu.make_async_copy(gate_hbm, gate_w, local_sem.at[1]),
+        pltpu.make_async_copy(up_hbm, up_w, local_sem.at[2]),
+        pltpu.make_async_copy(down_hbm, down_w, local_sem.at[3]),
+    ]
+
+    barrier = pltpu.get_barrier_semaphore()
+    for peer in (right, left, across):
+        pl.semaphore_signal(barrier, inc=1, device_id=peer, device_id_type=MESH)
+    pl.semaphore_wait(barrier, 3)
+
+    def slot(dz, dx):
+        return SLOT[(dz, dx)]
+
+    plan = {}
+
+    def add(name, src, dst, peer):
+        plan[name] = (src, dst, peer, len(plan))
+
+    def copy(name):
+        src, dst, peer, at = plan[name]
+        return pltpu.make_async_remote_copy(
+            src_ref=src, dst_ref=dst, send_sem=send_sem.at[at], recv_sem=recv_sem.at[at],
+            device_id=peer, device_id_type=MESH,
+        )
+
+    def tok(dz, dx, sel):
+        return tokens.at[slot(dz, dx), sel]
+
+    def res(dz, dx, sel):
+        return sums.at[slot(dz, dx), sel]
+
+    for i in range(4):
+        add(("r", 0, i), tok(0, 0, part[i]), tok(0, 3, part[i]), right)
+        add(("l", 0, i), tok(0, 0, part[i]), tok(0, 1, part[i]), left)
+    for i in range(2):
+        add(("r", 1, i), tok(1, 0, part[i]), tok(1, 3, part[i]), right)
+        add(("l", 1, i), tok(1, 0, part[i]), tok(1, 1, part[i]), left)
+    for dz, i in ((0, 0), (0, 2), (1, 0)):
+        add(("rr", dz, i), tok(dz, 3, part[i]), tok(dz, 2, part[i]), right)
+        add(("ll", dz, i + 1), tok(dz, 1, part[i + 1]), tok(dz, 2, part[i + 1]), left)
+    add(("z", 0, 0), tok(0, 0, low), tok(1, 0, low), across)
+    for dx in range(4):
+        add(("z", dx, 1), tok(0, dx, high), tok(1, dx, high), across)
+    for dz in range(2):
+        add(("fr", dz), res(dz, 2, part[0]), far_1.at[dz, 0], right)
+        add(("fl", dz), res(dz, 2, part[1]), far_1.at[dz, 1], left)
+        add(("nr", dz), res(dz, 1, low), near_1.at[dz, 0], right)
+        add(("nl", dz), res(dz, 3, low), near_1.at[dz, 1], left)
+    add("fr2", res(0, 2, part[2]), far_2.at[0], right)
+    add("fl2", res(0, 2, part[3]), far_2.at[1], left)
+    add("nr2", res(0, 1, high), near_2.at[0], right)
+    add("nl2", res(0, 3, high), near_2.at[1], left)
+    for dx in range(4):
+        add(("sz", dx), res(1, dx, high), cross_2.at[dx], across)
+    add("sz1", res(1, 0, low), cross_1, across)
+
+    def start(*names):
+        for name in names:
+            copy(name).start()
+
+    def arrived(*names):
+        for name in names:
+            copy(name).wait_recv()
+
+    def grow(dz, dx, sel, *terms):
+        ref = res(dz, dx, sel)
+        total = ref[...].astype(jnp.float32)
+        for term in terms:
+            total = total + term[...].astype(jnp.float32)
+        ref[...] = total.astype(jnp.bfloat16)
+
+    own.wait()
+    start(("z", 0, 0), ("r", 0, 2), ("l", 0, 3), ("r", 0, 3), ("l", 0, 2), ("z", 0, 1))
+    start(("r", 0, 0), ("l", 0, 1), ("r", 0, 1), ("l", 0, 0))
+    for load in loads:
+        load.start()
+
+    def step(at, carry):
+        @pl.when(at == 0)
+        def _():
+            for load in loads:
+                load.wait()
+
+        @pl.when(at == 1)
+        def _():
+            arrived(("r", 0, 2))
+            start(("rr", 0, 2))
+            arrived(("l", 0, 3))
+            start(("ll", 0, 3))
+            arrived(("l", 0, 2))
+            start(("z", 1, 1))
+            arrived(("r", 0, 0))
+            start(("rr", 0, 0))
+            arrived(("l", 0, 1))
+            start(("ll", 0, 1))
+            arrived(("z", 0, 0))
+            start(("r", 1, 0), ("l", 1, 1), ("r", 1, 1), ("l", 1, 0))
+            arrived(("z", 0, 1))
+
+        @pl.when(at == 2)
+        def _():
+            arrived(("rr", 0, 2), ("ll", 0, 3))
+            start(("z", 2, 1))
+            arrived(("r", 0, 3))
+            start(("z", 3, 1))
+            arrived(("l", 0, 0))
+
+        @pl.when(at == 3)
+        def _():
+            arrived(("r", 0, 1))
+
+        @pl.when(at == 4)
+        def _():
+            arrived(("r", 1, 0))
+            start(("rr", 1, 0))
+            arrived(("l", 1, 1))
+            start(("ll", 1, 1))
+            arrived(("rr", 0, 0), ("ll", 0, 1))
+
+        @pl.when(at == 5)
+        def _():
+            arrived(("l", 1, 0), ("z", 1, 1))
+
+        @pl.when(at == 6)
+        def _():
+            arrived(("rr", 1, 0), ("ll", 1, 1), ("z", 2, 1))
+
+        @pl.when(at == 7)
+        def _():
+            arrived(("r", 1, 1), ("z", 3, 1))
+
+        block = tokens[at]
+        width = gate_w.shape[1]
+        for col in range(0, width, 256):
+            cols = slice(col, min(col + 256, width))
+            gate_val = jnp.dot(block, gate_w[:, cols], preferred_element_type=jnp.float32)
+            up_val = jnp.dot(block, up_w[:, cols], preferred_element_type=jnp.float32)
+            act = gate_val / (1.0 + jnp.exp(-gate_val)) * up_val
+            hidden[:, cols] = act.astype(jnp.bfloat16)
+        held = hidden[...]
+        for col in range(0, down_w.shape[1], 512):
+            cols = slice(col, col + 512)
+            piece = jnp.dot(held, down_w[:, cols], preferred_element_type=jnp.float32)
+            sums[at, :, cols] = piece.astype(jnp.bfloat16)
+
+        @pl.when(at == 4)
+        def _():
+            start(("fr", 0), ("fl", 0))
+
+        @pl.when(at == 6)
+        def _():
+            start(("fr", 1), ("fl", 1), ("sz", 2), ("sz", 1))
+
+        @pl.when(at == 7)
+        def _():
+            start(("sz", 3), ("sz", 0))
+
+        return carry
+
+    lax.fori_loop(0, 8, step, 0)
+
+    for dz in range(2):
+        arrived(("fr", dz))
+        grow(dz, 1, part[0], far_1.at[dz, 0])
+        start(("nr", dz))
+        arrived(("fl", dz))
+        grow(dz, 3, part[1], far_1.at[dz, 1])
+        start(("nl", dz))
+    arrived(("sz", 2))
+    grow(0, 2, high, cross_2.at[2])
+    start("fr2", "fl2")
+    arrived(("sz", 1))
+    grow(0, 1, high, cross_2.at[1])
+    arrived(("nr", 0), ("nl", 0))
+    grow(0, 0, low, near_1.at[0, 0], near_1.at[0, 1])
+    arrived(("nr", 1), ("nl", 1))
+    grow(1, 0, low, near_1.at[1, 0], near_1.at[1, 1])
+    start("sz1")
+    arrived("fr2")
+    grow(0, 1, part[2], far_2.at[0])
+    start("nr2")
+    arrived(("sz", 3), "fl2")
+    grow(0, 3, high, cross_2.at[3])
+    grow(0, 3, part[3], far_2.at[1])
+    start("nl2")
+
+    def finish(sel, *terms):
+        total = res(0, 0, sel)[...].astype(jnp.float32)
+        for term in terms:
+            total = total + term[...].astype(jnp.float32)
+        out_ref[sel, :] = (resid_ref[sel, :] + total).astype(jnp.bfloat16)
+
+    arrived(("sz", 0), "nr2", "nl2")
+    finish(high, cross_2.at[0], near_2.at[0], near_2.at[1])
+    arrived("sz1")
+    finish(low, cross_1)
+    for name in plan:
+        copy(name).wait_send()
+
+
+def mlp_phase(normed, residual_sum, w_gate, w_up, w_down):
+    rows, width = normed.shape
+    half, quarter = rows // 2, rows // 4
+    ff = w_gate.shape[1]
+    anywhere = pl.BlockSpec(memory_space=pl.ANY)
+    vmem = pl.BlockSpec(memory_space=pltpu.VMEM)
+    bf16 = jnp.bfloat16
+    copies = 8 + 4 + 6 + 5 + 8 + 4 + 5
+    return pl.pallas_call(
+        mlp_kernel,
+        out_shape=jax.ShapeDtypeStruct((rows, width), bf16),
+        in_specs=[anywhere, vmem, anywhere, anywhere, anywhere],
+        out_specs=vmem,
+        scratch_shapes=[
+            pltpu.VMEM((8, rows, width), bf16),
+            pltpu.VMEM((width, ff), bf16),
+            pltpu.VMEM((width, ff), bf16),
+            pltpu.VMEM((ff, width), bf16),
+            pltpu.VMEM((rows, ff), bf16),
+            pltpu.VMEM((8, rows, width), bf16),
+            pltpu.VMEM((2, 2, quarter, width), bf16),
+            pltpu.VMEM((2, quarter, width), bf16),
+            pltpu.VMEM((2, 2, half, width), bf16),
+            pltpu.VMEM((2, half, width), bf16),
+            pltpu.VMEM((half, width), bf16),
+            pltpu.VMEM((4, half, width), bf16),
+            pltpu.SemaphoreType.DMA((4,)),
+            pltpu.SemaphoreType.DMA((copies,)),
+            pltpu.SemaphoreType.DMA((copies,)),
+        ],
+        compiler_params=pltpu.CompilerParams(
+            collective_id=1, has_side_effects=True, vmem_limit_bytes=67043328
+        ),
+        name="mlp_exchange",
+    )(normed, residual_sum, w_gate, w_up, w_down)
 
 
 def per_device(resid, query, keys, values, doc_lengths, w_out, norm_gain, w_gate, w_up, w_down):
@@ -142,15 +414,7 @@
     residual_sum = resid.astype(jnp.float32) + projected
     mean_sq = jnp.mean(residual_sum * residual_sum, axis=1, keepdims=True)
     normed = (residual_sum * lax.rsqrt(mean_sq + EPS) * norm_gain).astype(jnp.bfloat16)
-    piece_rows = lax.all_gather(normed, "dp", axis=0, tiled=True)
-    gate_val = jnp.dot(piece_rows, w_gate, preferred_element_type=jnp.float32)
-    up_val = jnp.dot(piece_rows, w_up, preferred_element_type=jnp.float32)
-    hidden_act = (jax.nn.silu(gate_val) * up_val).astype(jnp.bfloat16)
-    partial_rows = jnp.dot(hidden_act, w_down, preferred_element_type=jnp.float32)
-    mlp_out = lax.psum_scatter(
-        partial_rows.astype(jnp.bfloat16), "dp", scatter_dimension=0, tiled=True
-    ).astype(jnp.float32)
-    return (residual_sum + mlp_out).astype(jnp.bfloat16)
+    return mlp_phase(normed, residual_sum, w_gate, w_up, w_down)
 
 
 def solution(mesh):

time: 750 us -> 503 us (0.67)
  waiting for transfers between devices: 347 us -> 124 us
  Pallas kernels: 0 us -> 119 us
  matrix products: 96.2 us -> 25.2 us
  local copies, waits for them, and re-layouts: 83.5 us -> 13.1 us
    pallas_call x0 -> x1, Pallas kernels: none -> 119 us  [mlp_phase(): pl.pallas_call(mlp_kernel, out_shape=jax.ShapeDtypeStruct((rows, width),...]
    reduce_scatter x1 -> x0, waiting for transfers between devices: 113 us -> none  [per_device(): lax.psum_scatter(partial_rows.astype(jnp.bfloat16), 'dp', scatter_dimensi...]
    all_gather x1 -> x0, waiting for transfers between devices: 107 us -> none  [per_device(): piece_rows = lax.all_gather(normed, 'dp', axis=0, tiled=True)]
    dot_general x2 -> x0, matrix products: 41.3 us -> none  [the longest x1 26.7 us: per_device(): jnp.dot(hidden_act, w_down, preferred_element_type=jnp.float32)]
    squeeze x16, local copies, waits for them, and re-layouts: 26.7 us -> 2.16 us  [online_update(): value_rows.reshape(value_rows.shape[0], kv_heads, head_dim)]
    squeeze x16, local copies, waits for them, and re-layouts: 26.6 us -> 2.11 us  [online_update(): key_rows.reshape(key_rows.shape[0], kv_heads, head_dim).transpose(1, 0, 2)]
    dot_general x17, matrix products: 22.7 us -> 5.85 us  [online_update(): jnp.einsum('aqd,akd->aqk', q_group, key_heads, preferred_element_type=jnp...]
    dot_general x17, matrix products: 26.6 us -> 12.2 us  [online_update(): jnp.einsum('aqk,akd->aqd', weights.astype(jnp.bfloat16), value_heads, pre...]
  transfers between devices with their start and end apart: 19 -> 17, of which waited for: 19 -> 17; matrix products, arithmetic and copies ran while one was open for 0% -> 1% of each run, Pallas kernels for 0% -> 0%
where the time goes in v1:
time: 503 us; the launch traced here: 500 us
  waiting for transfers between devices  124 us (25%)
  Pallas kernels  119 us (24%)
  starting transfers between devices  99.8 us (20%)
  blocking collectives  90 us (18%)
  matrix products  25.2 us (5%)
  between operations  13.6 us (3%)
  local copies, waits for them, and re-layouts  13.1 us (3%)
  other arithmetic  12.8 us (3%)
    pallas_call x1, Pallas kernels, mlp_phase(): pl.pallas_call(mlp_kernel, out_shape=jax.ShapeDtypeStruct((rows, width),...  119 us
    reduce_scatter x1, waiting for transfers between devices, per_device(): lax.psum_scatter(jnp.dot(spread, w_out, preferred_element_type=jnp.float3...  110 us
    ppermute x16, starting transfers between devices, from_behind(): return lax.ppermute(block, axis, route)  99.8 us
    all_to_all x1, blocking collectives, per_device(): lax.all_to_all(heads_out, 'dp', split_axis=1, concat_axis=0, tiled=True)  90 us
    ppermute x16, waiting for transfers between devices, from_behind(): return lax.ppermute(block, axis, route)  14.3 us
    dot_general x17, matrix products, online_update(): jnp.einsum('aqk,akd->aqd', weights.astype(jnp.bfloat16), value_heads, pre...  12.2 us
  transfers between devices with their start and end apart: 17, of which 17 were waited for; matrix products, arithmetic and copies ran while one was open for 1% of the time, Pallas kernels for 0%

profile of v1, /device:TPU:0, one launch (start us, length us, event | category | flops | bytes accessed | tf_op | source)
XLA Modules:
  0.0 500.1 jit_solution(12557316654643351051)
XLA Ops:
  14.2 145.0 %while.22 = (s32[]{:T(128)}, f32[4,512]{1,0:T(4,128)S(1)}, f32[4,512]{1,0:T(4,128)S(1)}, f32[4,512,128]{2,1,0:T(8,128)S(1)}, bf16[2,128,512]{1,2,0:T(8,128)(2,1)...) while((s32[]{:T(128)}, f32[4,512]{1,0:T(4,128)S(1)}, ...), condition=%wide.region_7.8_spmd.clone, body=%wide.region_4.7_spmd.clone.sunk | while | flops 137154816 | bytes 9210569 | solution.py:401
  14.2 1.3 collective-permute-start
  18.3 6.5 %collective-permute-start = (bf16[2,128,512]{1,2,0:T(8,128)(2,1)S(1)}, bf16[2,128,512]{1,2,0:T(8,128)(2,1)S(1)}, u32[]{:S(2)}, u32[]{:S(2)}) collective-permute-start(bf16[2,128,512]{1,2,0:T(8,128)(2,1)S(1)} %get-tuple-element.393), channel_id=1, source_target_pairs={{0,1},{1,2},{2,3},{3,4},{4,5},{5,6},{6,7},{7,8},{8,9},{9,10},{10,1... | collective-permute-start | bytes 786440 | tf_op jit(solution)/shard_map/while/body/eval_jaxpr/ppermute | solution.py:21
  27.6 6.5 %collective-permute-start = (bf16[2,128,512]{1,2,0:T(8,128)(2,1)S(1)}, bf16[2,128,512]{1,2,0:T(8,128)(2,1)S(1)}, u32[]{:S(2)}, u32[]{:S(2)}) collective-permute-start(bf16[2,128,512]{1,2,0:T(8,128)(2,1)S(1)} %get-tuple-element.393), channel_id=1, source_target_pairs={{0,1},{1,2},{2,3},{3,4},{4,5},{5,6},{6,7},{7,8},{8,9},{9,10},{10,1... | collective-permute-start | bytes 786440 | tf_op jit(solution)/shard_map/while/body/eval_jaxpr/ppermute | solution.py:21
  37.0 6.6 %collective-permute-start = (bf16[2,128,512]{1,2,0:T(8,128)(2,1)S(1)}, bf16[2,128,512]{1,2,0:T(8,128)(2,1)S(1)}, u32[]{:S(2)}, u32[]{:S(2)}) collective-permute-start(bf16[2,128,512]{1,2,0:T(8,128)(2,1)S(1)} %get-tuple-element.393), channel_id=1, source_target_pairs={{0,1},{1,2},{2,3},{3,4},{4,5},{5,6},{6,7},{7,8},{8,9},{9,10},{10,1... | collective-permute-start | bytes 786440 | tf_op jit(solution)/shard_map/while/body/eval_jaxpr/ppermute | solution.py:21
  46.4 6.5 %collective-permute-start = (bf16[2,128,512]{1,2,0:T(8,128)(2,1)S(1)}, bf16[2,128,512]{1,2,0:T(8,128)(2,1)S(1)}, u32[]{:S(2)}, u32[]{:S(2)}) collective-permute-start(bf16[2,128,512]{1,2,0:T(8,128)(2,1)S(1)} %get-tuple-element.393), channel_id=1, source_target_pairs={{0,1},{1,2},{2,3},{3,4},{4,5},{5,6},{6,7},{7,8},{8,9},{9,10},{10,1... | collective-permute-start | bytes 786440 | tf_op jit(solution)/shard_map/while/body/eval_jaxpr/ppermute | solution.py:21
  55.7 6.6 %collective-permute-start = (bf16[2,128,512]{1,2,0:T(8,128)(2,1)S(1)}, bf16[2,128,512]{1,2,0:T(8,128)(2,1)S(1)}, u32[]{:S(2)}, u32[]{:S(2)}) collective-permute-start(bf16[2,128,512]{1,2,0:T(8,128)(2,1)S(1)} %get-tuple-element.393), channel_id=1, source_target_pairs={{0,1},{1,2},{2,3},{3,4},{4,5},{5,6},{6,7},{7,8},{8,9},{9,10},{10,1... | collective-permute-start | bytes 786440 | tf_op jit(solution)/shard_map/while/body/eval_jaxpr/ppermute | solution.py:21
  65.1 6.5 %collective-permute-start = (bf16[2,128,512]{1,2,0:T(8,128)(2,1)S(1)}, bf16[2,128,512]{1,2,0:T(8,128)(2,1)S(1)}, u32[]{:S(2)}, u32[]{:S(2)}) collective-permute-start(bf16[2,128,512]{1,2,0:T(8,128)(2,1)S(1)} %get-tuple-element.393), channel_id=1, source_target_pairs={{0,1},{1,2},{2,3},{3,4},{4,5},{5,6},{6,7},{7,8},{8,9},{9,10},{10,1... | collective-permute-start | bytes 786440 | tf_op jit(solution)/shard_map/while/body/eval_jaxpr/ppermute | solution.py:21
  74.5 6.6 %collective-permute-start = (bf16[2,128,512]{1,2,0:T(8,128)(2,1)S(1)}, bf16[2,128,512]{1,2,0:T(8,128)(2,1)S(1)}, u32[]{:S(2)}, u32[]{:S(2)}) collective-permute-start(bf16[2,128,512]{1,2,0:T(8,128)(2,1)S(1)} %get-tuple-element.393), channel_id=1, source_target_pairs={{0,1},{1,2},{2,3},{3,4},{4,5},{5,6},{6,7},{7,8},{8,9},{9,10},{10,1... | collective-permute-start | bytes 786440 | tf_op jit(solution)/shard_map/while/body/eval_jaxpr/ppermute | solution.py:21
  83.9 6.5 %collective-permute-start = (bf16[2,128,512]{1,2,0:T(8,128)(2,1)S(1)}, bf16[2,128,512]{1,2,0:T(8,128)(2,1)S(1)}, u32[]{:S(2)}, u32[]{:S(2)}) collective-permute-start(bf16[2,128,512]{1,2,0:T(8,128)(2,1)S(1)} %get-tuple-element.393), channel_id=1, source_target_pairs={{0,1},{1,2},{2,3},{3,4},{4,5},{5,6},{6,7},{7,8},{8,9},{9,10},{10,1... | collective-permute-start | bytes 786440 | tf_op jit(solution)/shard_map/while/body/eval_jaxpr/ppermute | solution.py:21
  93.2 6.6 %collective-permute-start = (bf16[2,128,512]{1,2,0:T(8,128)(2,1)S(1)}, bf16[2,128,512]{1,2,0:T(8,128)(2,1)S(1)}, u32[]{:S(2)}, u32[]{:S(2)}) collective-permute-start(bf16[2,128,512]{1,2,0:T(8,128)(2,1)S(1)} %get-tuple-element.393), channel_id=1, source_target_pairs={{0,1},{1,2},{2,3},{3,4},{4,5},{5,6},{6,7},{7,8},{8,9},{9,10},{10,1... | collective-permute-start | bytes 786440 | tf_op jit(solution)/shard_map/while/body/eval_jaxpr/ppermute | solution.py:21
  102.6 6.5 %collective-permute-start = (bf16[2,128,512]{1,2,0:T(8,128)(2,1)S(1)}, bf16[2,128,512]{1,2,0:T(8,128)(2,1)S(1)}, u32[]{:S(2)}, u32[]{:S(2)}) collective-permute-start(bf16[2,128,512]{1,2,0:T(8,128)(2,1)S(1)} %get-tuple-element.393), channel_id=1, source_target_pairs={{0,1},{1,2},{2,3},{3,4},{4,5},{5,6},{6,7},{7,8},{8,9},{9,10},{10,1... | collective-permute-start | bytes 786440 | tf_op jit(solution)/shard_map/while/body/eval_jaxpr/ppermute | solution.py:21
  112.0 6.6 %collective-permute-start = (bf16[2,128,512]{1,2,0:T(8,128)(2,1)S(1)}, bf16[2,128,512]{1,2,0:T(8,128)(2,1)S(1)}, u32[]{:S(2)}, u32[]{:S(2)}) collective-permute-start(bf16[2,128,512]{1,2,0:T(8,128)(2,1)S(1)} %get-tuple-element.393), channel_id=1, source_target_pairs={{0,1},{1,2},{2,3},{3,4},{4,5},{5,6},{6,7},{7,8},{8,9},{9,10},{10,1... | collective-permute-start | bytes 786440 | tf_op jit(solution)/shard_map/while/body/eval_jaxpr/ppermute | solution.py:21
  121.4 6.5 %collective-permute-start = (bf16[2,128,512]{1,2,0:T(8,128)(2,1)S(1)}, bf16[2,128,512]{1,2,0:T(8,128)(2,1)S(1)}, u32[]{:S(2)}, u32[]{:S(2)}) collective-permute-start(bf16[2,128,512]{1,2,0:T(8,128)(2,1)S(1)} %get-tuple-element.393), channel_id=1, source_target_pairs={{0,1},{1,2},{2,3},{3,4},{4,5},{5,6},{6,7},{7,8},{8,9},{9,10},{10,1... | collective-permute-start | bytes 786440 | tf_op jit(solution)/shard_map/while/body/eval_jaxpr/ppermute | solution.py:21
  130.8 6.6 %collective-permute-start = (bf16[2,128,512]{1,2,0:T(8,128)(2,1)S(1)}, bf16[2,128,512]{1,2,0:T(8,128)(2,1)S(1)}, u32[]{:S(2)}, u32[]{:S(2)}) collective-permute-start(bf16[2,128,512]{1,2,0:T(8,128)(2,1)S(1)} %get-tuple-element.393), channel_id=1, source_target_pairs={{0,1},{1,2},{2,3},{3,4},{4,5},{5,6},{6,7},{7,8},{8,9},{9,10},{10,1... | collective-permute-start | bytes 786440 | tf_op jit(solution)/shard_map/while/body/eval_jaxpr/ppermute | solution.py:21
  140.2 6.5 %collective-permute-start = (bf16[2,128,512]{1,2,0:T(8,128)(2,1)S(1)}, bf16[2,128,512]{1,2,0:T(8,128)(2,1)S(1)}, u32[]{:S(2)}, u32[]{:S(2)}) collective-permute-start(bf16[2,128,512]{1,2,0:T(8,128)(2,1)S(1)} %get-tuple-element.393), channel_id=1, source_target_pairs={{0,1},{1,2},{2,3},{3,4},{4,5},{5,6},{6,7},{7,8},{8,9},{9,10},{10,1... | collective-permute-start | bytes 786440 | tf_op jit(solution)/shard_map/while/body/eval_jaxpr/ppermute | solution.py:21
  149.5 6.8 %collective-permute-start = (bf16[2,128,512]{1,2,0:T(8,128)(2,1)S(1)}, bf16[2,128,512]{1,2,0:T(8,128)(2,1)S(1)}, u32[]{:S(2)}, u32[]{:S(2)}) collective-permute-start(bf16[2,128,512]{1,2,0:T(8,128)(2,1)S(1)} %get-tuple-element.393), channel_id=1, source_target_pairs={{0,1},{1,2},{2,3},{3,4},{4,5},{5,6},{6,7},{7,8},{8,9},{9,10},{10,1... | collective-permute-start | bytes 786440 | tf_op jit(solution)/shard_map/while/body/eval_jaxpr/ppermute | solution.py:21
  159.8 90.0 %all_to_all.16 = bf16[128,8,256]{0,2,1:T(8,128)(2,1)S(1)} all-to-all(bf16[128,8,256]{0,2,1:T(8,128)(2,1)S(1)} %bitcast.84), channel_id=1, replica_groups=mesh['dp'=8,'ctx'=16] {'dp'}, dimensions={1} | all-to-all | bytes 1048576 | tf_op jit(solution)/shard_map/all_to_all | solution.py:407
  250.0 7.2 %convolution_convert_fusion = bf16[1024,4096]{1,0:T(8,128)(2,1)} fusion(bf16[1024,256]{1,0:T(8,128)(2,1)S(1)} %bitcast.86, bf16[256,4096]{1,0:T(8,128)(2,1)} %param.17), kind=kOutput, calls=%fused_computation.20 | convolution fusion | flops 2151677952 | bytes 11010048 | tf_op jit(solution)/shard_map/dot_general | solution.py:409
  257.2 110.0 %reduce-scatter.2.cloned.1.call-done = bf16[128,4096]{1,0:T(8,128)(2,1)} async-done(((bf16[1024,4096]{1,0:T(8,128)(2,1)}), bf16[128,4096]{1,0:T(8,128)(2,1)}) %reduce-scatter.2.cloned.1.call-update) | async-done | bytes 1048592 | tf_op jit(solution)/shard_map/reduce_scatter | solution.py:408
  367.2 3.0 convert_add_fusion
  370.3 1.4 multiply_convert_fusion.normed_ref
  371.6 119.3 %mlp_exchange.1 = bf16[128,4096]{1,0:T(8,128)(2,1)} custom-call(bf16[128,4096]{1,0:T(8,128)(2,1)} %multiply_convert_fusion.normed_ref, f32[128,4096]{1,0:T(8,128)} %get-tuple-element.296.resid_ref, bf16[4096,896]{1,0:T(8,128)(2,1)} %gate_hbm.1, bf16[4096,896]{1,0:T(8,128)(2,1)} %up_hbm.1, bf16[896,4096]{1,0:T(8,128)(2,1)} %down_hbm.1), custom_call_target="tpu_custom_call" | custom-call | tf_op jit(solution)/shard_map/mlp_exchange/pallas_call | solution.py:324
  490.9 2.3 copy.97
  (303 shorter events, 51.6 us)
Async XLA Ops:
  6.5 5.0 copy-start.2
  6.5 360.7 %reduce-scatter.2.cloned.1.call-start = ((), (), s32[]{:S(2)}) async-start(), calls=%async_computation.2 | async-start | bytes 9437184 | tf_op jit(solution)/shard_map/reduce_scatter | solution.py:408
  12.6 0.9 copy-start.3
  14.2 2.4 collective-permute-start
  18.3 7.6 %collective-permute-start = (bf16[2,128,512]{1,2,0:T(8,128)(2,1)S(1)}, bf16[2,128,512]{1,2,0:T(8,128)(2,1)S(1)}, u32[]{:S(2)}, u32[]{:S(2)}) collective-permute-start(bf16[2,128,512]{1,2,0:T(8,128)(2,1)S(1)} %get-tuple-element.393), channel_id=1, source_target_pairs={{0,1},{1,2},{2,3},{3,4},{4,5},{5,6},{6,7},{7,8},{8,9},{9,10},{10,1... | collective-permute-start | bytes 786440 | tf_op jit(solution)/shard_map/while/body/eval_jaxpr/ppermute | solution.py:21
  27.6 7.7 %collective-permute-start = (bf16[2,128,512]{1,2,0:T(8,128)(2,1)S(1)}, bf16[2,128,512]{1,2,0:T(8,128)(2,1)S(1)}, u32[]{:S(2)}, u32[]{:S(2)}) collective-permute-start(bf16[2,128,512]{1,2,0:T(8,128)(2,1)S(1)} %get-tuple-element.393), channel_id=1, source_target_pairs={{0,1},{1,2},{2,3},{3,4},{4,5},{5,6},{6,7},{7,8},{8,9},{9,10},{10,1... | collective-permute-start | bytes 786440 | tf_op jit(solution)/shard_map/while/body/eval_jaxpr/ppermute | solution.py:21
  37.0 7.7 %collective-permute-start = (bf16[2,128,512]{1,2,0:T(8,128)(2,1)S(1)}, bf16[2,128,512]{1,2,0:T(8,128)(2,1)S(1)}, u32[]{:S(2)}, u32[]{:S(2)}) collective-permute-start(bf16[2,128,512]{1,2,0:T(8,128)(2,1)S(1)} %get-tuple-element.393), channel_id=1, source_target_pairs={{0,1},{1,2},{2,3},{3,4},{4,5},{5,6},{6,7},{7,8},{8,9},{9,10},{10,1... | collective-permute-start | bytes 786440 | tf_op jit(solution)/shard_map/while/body/eval_jaxpr/ppermute | solution.py:21
  46.4 7.7 %collective-permute-start = (bf16[2,128,512]{1,2,0:T(8,128)(2,1)S(1)}, bf16[2,128,512]{1,2,0:T(8,128)(2,1)S(1)}, u32[]{:S(2)}, u32[]{:S(2)}) collective-permute-start(bf16[2,128,512]{1,2,0:T(8,128)(2,1)S(1)} %get-tuple-element.393), channel_id=1, source_target_pairs={{0,1},{1,2},{2,3},{3,4},{4,5},{5,6},{6,7},{7,8},{8,9},{9,10},{10,1... | collective-permute-start | bytes 786440 | tf_op jit(solution)/shard_map/while/body/eval_jaxpr/ppermute | solution.py:21
  55.7 7.7 %collective-permute-start = (bf16[2,128,512]{1,2,0:T(8,128)(2,1)S(1)}, bf16[2,128,512]{1,2,0:T(8,128)(2,1)S(1)}, u32[]{:S(2)}, u32[]{:S(2)}) collective-permute-start(bf16[2,128,512]{1,2,0:T(8,128)(2,1)S(1)} %get-tuple-element.393), channel_id=1, source_target_pairs={{0,1},{1,2},{2,3},{3,4},{4,5},{5,6},{6,7},{7,8},{8,9},{9,10},{10,1... | collective-permute-start | bytes 786440 | tf_op jit(solution)/shard_map/while/body/eval_jaxpr/ppermute | solution.py:21
  65.1 7.7 %collective-permute-start = (bf16[2,128,512]{1,2,0:T(8,128)(2,1)S(1)}, bf16[2,128,512]{1,2,0:T(8,128)(2,1)S(1)}, u32[]{:S(2)}, u32[]{:S(2)}) collective-permute-start(bf16[2,128,512]{1,2,0:T(8,128)(2,1)S(1)} %get-tuple-element.393), channel_id=1, source_target_pairs={{0,1},{1,2},{2,3},{3,4},{4,5},{5,6},{6,7},{7,8},{8,9},{9,10},{10,1... | collective-permute-start | bytes 786440 | tf_op jit(solution)/shard_map/while/body/eval_jaxpr/ppermute | solution.py:21
  74.5 7.7 %collective-permute-start = (bf16[2,128,512]{1,2,0:T(8,128)(2,1)S(1)}, bf16[2,128,512]{1,2,0:T(8,128)(2,1)S(1)}, u32[]{:S(2)}, u32[]{:S(2)}) collective-permute-start(bf16[2,128,512]{1,2,0:T(8,128)(2,1)S(1)} %get-tuple-element.393), channel_id=1, source_target_pairs={{0,1},{1,2},{2,3},{3,4},{4,5},{5,6},{6,7},{7,8},{8,9},{9,10},{10,1... | collective-permute-start | bytes 786440 | tf_op jit(solution)/shard_map/while/body/eval_jaxpr/ppermute | solution.py:21
  83.9 7.7 %collective-permute-start = (bf16[2,128,512]{1,2,0:T(8,128)(2,1)S(1)}, bf16[2,128,512]{1,2,0:T(8,128)(2,1)S(1)}, u32[]{:S(2)}, u32[]{:S(2)}) collective-permute-start(bf16[2,128,512]{1,2,0:T(8,128)(2,1)S(1)} %get-tuple-element.393), channel_id=1, source_target_pairs={{0,1},{1,2},{2,3},{3,4},{4,5},{5,6},{6,7},{7,8},{8,9},{9,10},{10,1... | collective-permute-start | bytes 786440 | tf_op jit(solution)/shard_map/while/body/eval_jaxpr/ppermute | solution.py:21
  93.2 7.7 %collective-permute-start = (bf16[2,128,512]{1,2,0:T(8,128)(2,1)S(1)}, bf16[2,128,512]{1,2,0:T(8,128)(2,1)S(1)}, u32[]{:S(2)}, u32[]{:S(2)}) collective-permute-start(bf16[2,128,512]{1,2,0:T(8,128)(2,1)S(1)} %get-tuple-element.393), channel_id=1, source_target_pairs={{0,1},{1,2},{2,3},{3,4},{4,5},{5,6},{6,7},{7,8},{8,9},{9,10},{10,1... | collective-permute-start | bytes 786440 | tf_op jit(solution)/shard_map/while/body/eval_jaxpr/ppermute | solution.py:21
  102.6 7.7 %collective-permute-start = (bf16[2,128,512]{1,2,0:T(8,128)(2,1)S(1)}, bf16[2,128,512]{1,2,0:T(8,128)(2,1)S(1)}, u32[]{:S(2)}, u32[]{:S(2)}) collective-permute-start(bf16[2,128,512]{1,2,0:T(8,128)(2,1)S(1)} %get-tuple-element.393), channel_id=1, source_target_pairs={{0,1},{1,2},{2,3},{3,4},{4,5},{5,6},{6,7},{7,8},{8,9},{9,10},{10,1... | collective-permute-start | bytes 786440 | tf_op jit(solution)/shard_map/while/body/eval_jaxpr/ppermute | solution.py:21
  112.0 7.7 %collective-permute-start = (bf16[2,128,512]{1,2,0:T(8,128)(2,1)S(1)}, bf16[2,128,512]{1,2,0:T(8,128)(2,1)S(1)}, u32[]{:S(2)}, u32[]{:S(2)}) collective-permute-start(bf16[2,128,512]{1,2,0:T(8,128)(2,1)S(1)} %get-tuple-element.393), channel_id=1, source_target_pairs={{0,1},{1,2},{2,3},{3,4},{4,5},{5,6},{6,7},{7,8},{8,9},{9,10},{10,1... | collective-permute-start | bytes 786440 | tf_op jit(solution)/shard_map/while/body/eval_jaxpr/ppermute | solution.py:21
  121.4 7.7 %collective-permute-start = (bf16[2,128,512]{1,2,0:T(8,128)(2,1)S(1)}, bf16[2,128,512]{1,2,0:T(8,128)(2,1)S(1)}, u32[]{:S(2)}, u32[]{:S(2)}) collective-permute-start(bf16[2,128,512]{1,2,0:T(8,128)(2,1)S(1)} %get-tuple-element.393), channel_id=1, source_target_pairs={{0,1},{1,2},{2,3},{3,4},{4,5},{5,6},{6,7},{7,8},{8,9},{9,10},{10,1... | collective-permute-start | bytes 786440 | tf_op jit(solution)/shard_map/while/body/eval_jaxpr/ppermute | solution.py:21
  130.8 7.7 %collective-permute-start = (bf16[2,128,512]{1,2,0:T(8,128)(2,1)S(1)}, bf16[2,128,512]{1,2,0:T(8,128)(2,1)S(1)}, u32[]{:S(2)}, u32[]{:S(2)}) collective-permute-start(bf16[2,128,512]{1,2,0:T(8,128)(2,1)S(1)} %get-tuple-element.393), channel_id=1, source_target_pairs={{0,1},{1,2},{2,3},{3,4},{4,5},{5,6},{6,7},{7,8},{8,9},{9,10},{10,1... | collective-permute-start | bytes 786440 | tf_op jit(solution)/shard_map/while/body/eval_jaxpr/ppermute | solution.py:21
  140.2 7.7 %collective-permute-start = (bf16[2,128,512]{1,2,0:T(8,128)(2,1)S(1)}, bf16[2,128,512]{1,2,0:T(8,128)(2,1)S(1)}, u32[]{:S(2)}, u32[]{:S(2)}) collective-permute-start(bf16[2,128,512]{1,2,0:T(8,128)(2,1)S(1)} %get-tuple-element.393), channel_id=1, source_target_pairs={{0,1},{1,2},{2,3},{3,4},{4,5},{5,6},{6,7},{7,8},{8,9},{9,10},{10,1... | collective-permute-start | bytes 786440 | tf_op jit(solution)/shard_map/while/body/eval_jaxpr/ppermute | solution.py:21
  149.5 8.0 %collective-permute-start = (bf16[2,128,512]{1,2,0:T(8,128)(2,1)S(1)}, bf16[2,128,512]{1,2,0:T(8,128)(2,1)S(1)}, u32[]{:S(2)}, u32[]{:S(2)}) collective-permute-start(bf16[2,128,512]{1,2,0:T(8,128)(2,1)S(1)} %get-tuple-element.393), channel_id=1, source_target_pairs={{0,1},{1,2},{2,3},{3,4},{4,5},{5,6},{6,7},{7,8},{8,9},{9,10},{10,1... | collective-permute-start | bytes 786440 | tf_op jit(solution)/shard_map/while/body/eval_jaxpr/ppermute | solution.py:21
  257.2 110.1 %copy-start = (bf16[128,4096]{1,0:T(8,128)(2,1)S(1)}, bf16[128,4096]{1,0:T(8,128)(2,1)}, u32[]{:S(2)}) copy-start(bf16[128,4096]{1,0:T(8,128)(2,1)} %param.12) | copy-start | bytes 3145732
  257.2 113.0 %copy-start.4 = (f32[4096]{0:T(1024)S(1)}, f32[4096]{0:T(1024)}, u32[]{:S(2)}) copy-start(f32[4096]{0:T(1024)} %param.18) | copy-start | bytes 49156
  367.2 3.0 copy-start.1
Sparse Core Ops, SparseCore 0:
  257.3 109.8 reduce-scatter.1

commit v2 on v1

--- a/solution.py
+++ b/solution.py
@@ -13,12 +13,6 @@
 ROPE_BASE = 500000.0
 EPS = 1e-05
 NEG_FILL = -1e30
-
-
-def from_behind(block, axis, distance):
-    devices = range(lax.axis_size(axis))
-    route = [(i - distance, i) for i in devices if i - distance in devices]
-    return lax.ppermute(block, axis, route)
 
 
 def rope_tables(rel_pos, head_dim):
@@ -49,35 +43,6 @@
     starts = doc_ends - doc_lengths
     inside = starts[None, :] <= positions[:, None]
     return jnp.max(jnp.where(inside, starts[None, :], 0), axis=1)
-
-
-def online_update(
-    softmax_state, q_group, key_rows, value_rows, key_pos, query_pos, query_start, score_scale
-):
-    row_max, row_sum, weighted = softmax_state
-    kv_heads = q_group.shape[0]
-    head_dim = q_group.shape[2]
-    key_heads = key_rows.reshape(key_rows.shape[0], kv_heads, head_dim).transpose(1, 0, 2)
-    value_heads = value_rows.reshape(value_rows.shape[0], kv_heads, head_dim).transpose(1, 0, 2)
-    scores = (
-        jnp.einsum("aqd,akd->aqk", q_group, key_heads, preferred_element_type=jnp.float32)
-        * score_scale
-    )
-    allowed = (key_pos[None, :] >= query_start[:, None]) & (key_pos[None, :] <= query_pos[:, None])
-    group_size = q_group.shape[1] // query_pos.shape[0]
-    allowed = jnp.tile(allowed, (group_size, 1))[None]
-    scores = jnp.where(allowed, scores, NEG_FILL)
-    new_max = jnp.maximum(row_max, jnp.max(scores, axis=-1))
-    weights = jnp.where(allowed, jnp.exp(scores - new_max[..., None]), 0.0)
-    factor = jnp.exp(row_max - new_max)
-    row_sum = row_sum * factor + jnp.sum(weights, axis=-1)
-    weighted = weighted * factor[..., None] + jnp.einsum(
-        "aqk,akd->aqd",
-        weights.astype(jnp.bfloat16),
-        value_heads,
-        preferred_element_type=jnp.float32,
-    )
-    return (new_max, row_sum, weighted)
 
 
 MESH = pl.DeviceIdType.MESH
@@ -350,15 +315,133 @@
     )(normed, residual_sum, w_gate, w_up, w_down)
 
 
+REACH = 16
+
+
+def attention_kernel(
+    q_ref, k_ref, v_ref, start_ref, out_ref,
+    slots, q_rows, row_max, sums, weighted, send_sem, recv_sem,
+):
+    ctx_count = lax.axis_size("ctx")
+    total = lax.axis_size("dp") * ctx_count
+    me = lax.axis_index("dp") * ctx_count + lax.axis_index("ctx")
+    ahead = (me + 1) % total
+    behind = (me + total - 1) % total
+    rows = k_ref.shape[0]
+    kv_heads, group_rows, head_dim = q_rows.shape
+    group = group_rows // rows
+    scale = 1.0 / math.sqrt(head_dim)
+    barrier = pltpu.get_barrier_semaphore()
+    pl.semaphore_signal(
+        barrier, inc=1, device_id=(behind // ctx_count, behind % ctx_count), device_id_type=MESH
+    )
+    slots[0, 0] = k_ref[...]
+    slots[0, 1] = v_ref[...]
+    received = jnp.minimum(me, REACH)
+    sent = jnp.where(me == total - 1, 0, jnp.minimum(me + 1, REACH))
+
+    def onward(t):
+        return pltpu.make_async_remote_copy(
+            src_ref=slots.at[t], dst_ref=slots.at[t + 1],
+            send_sem=send_sem.at[t], recv_sem=recv_sem.at[t],
+            device_id=(ahead // ctx_count, ahead % ctx_count), device_id_type=MESH,
+        )
+
+    pl.semaphore_wait(barrier, 1)
+
+    @pl.when(sent > 0)
+    def _():
+        onward(0).start()
+
+    for h in range(kv_heads):
+        for g in range(group):
+            at = (h * group + g) * head_dim
+            q_rows[h, g * rows:(g + 1) * rows, :] = q_ref[:, at:at + head_dim]
+    row_max[...] = jnp.full(row_max.shape, NEG_FILL, jnp.float32)
+    sums[...] = jnp.zeros(sums.shape, jnp.float32)
+    weighted[...] = jnp.zeros(weighted.shape, jnp.float32)
+
+    def step(t, carry):
+        @pl.when(t > 0)
+        def _():
+            onward(t - 1).wait_recv()
+
+        @pl.when((t > 0) & (t < sent))
+        def _():
+            onward(t).start()
+
+        key_at = (me - t) * rows + lax.broadcasted_iota(jnp.int32, (rows, rows), 1)
+        query_at = me * rows + lax.broadcasted_iota(jnp.int32, (rows, rows), 0)
+        allowed = (key_at >= start_ref[...]) & (key_at <= query_at)
+        for h in range(kv_heads):
+            cols = slice(h * head_dim, (h + 1) * head_dim)
+            scores = lax.dot_general(
+                q_rows[h], slots[t, 0, :, cols], (((1,), (1,)), ((), ())),
+                preferred_element_type=jnp.float32,
+            )
+            scores = jnp.where(
+                allowed[None], (scores * scale).reshape(group, rows, rows), NEG_FILL
+            ).reshape(group_rows, rows)
+            old_max = row_max[h]
+            new_max = jnp.maximum(old_max, jnp.max(scores, axis=-1, keepdims=True))
+            weights = jnp.exp(scores - new_max)
+            factor = jnp.exp(old_max - new_max)
+            row_max[h] = new_max
+            sums[h] = sums[h] * factor + weights
+            weighted[h] = weighted[h] * factor + jnp.dot(
+                weights.astype(jnp.bfloat16), slots[t, 1, :, cols],
+                preferred_element_type=jnp.float32,
+            )
+        return carry
+
+    lax.fori_loop(0, received + 1, step, 0)
+    for h in range(kv_heads):
+        head_rows = weighted[h] / jnp.sum(sums[h], axis=-1, keepdims=True)
+        for g in range(group):
+            at = (h * group + g) * head_dim
+            out_ref[:, at:at + head_dim] = head_rows[g * rows:(g + 1) * rows].astype(jnp.bfloat16)
+
+    def drain(t, carry):
+        onward(t).wait_send()
+        return carry
+
+    lax.fori_loop(0, sent, drain, 0)
+
+
+def attention_phase(q_rot, k_rot, values, query_start):
+    rows, width = q_rot.shape
+    kv_width = k_rot.shape[1]
+    kv_heads = kv_width // HEAD_DIM
+    group_rows = width // kv_width * rows
+    vmem = pl.BlockSpec(memory_space=pltpu.VMEM)
+    per_row = (kv_heads, group_rows, HEAD_DIM)
+    starts = jnp.broadcast_to(query_start[:, None], (rows, rows))
+    return pl.pallas_call(
+        attention_kernel,
+        out_shape=jax.ShapeDtypeStruct((rows, width), jnp.bfloat16),
+        in_specs=[vmem, vmem, vmem, vmem],
+        out_specs=vmem,
+        scratch_shapes=[
+            pltpu.VMEM((REACH + 1, 2, rows, kv_width), jnp.bfloat16),
+            pltpu.VMEM(per_row, jnp.bfloat16),
+            pltpu.VMEM(per_row, jnp.float32),
+            pltpu.VMEM(per_row, jnp.float32),
+            pltpu.VMEM(per_row, jnp.float32),
+            pltpu.SemaphoreType.DMA((REACH,)),
+            pltpu.SemaphoreType.DMA((REACH,)),
+        ],
+        compiler_params=pltpu.CompilerParams(
+            collective_id=2, has_side_effects=True, vmem_limit_bytes=33554432
+        ),
+        name="attention_chain",
+    )(q_rot, k_rot, values, starts)
+
+
 def per_device(resid, query, keys, values, doc_lengths, w_out, norm_gain, w_gate, w_up, w_down):
     tok_rows = resid.shape[0]
-    dp_count = lax.axis_size("dp")
-    ctx_count = lax.axis_size("ctx")
-    reach_devs = min(16, dp_count * ctx_count // 4)
     head_dim = HEAD_DIM
     kv_heads = keys.shape[1] // head_dim
     num_heads = query.shape[1] // head_dim
-    group_size = num_heads // kv_heads
     my_block = lax.axis_index(("dp", "ctx"))
     local_index = jnp.arange(tok_rows, dtype=jnp.int32)
     query_pos = my_block * tok_rows + local_index
@@ -366,44 +449,7 @@
     cosine, sine_val = rope_tables(query_pos - query_start, head_dim)
     q_rot = rotate(query, cosine, sine_val, num_heads, head_dim)
     k_rot = rotate(keys, cosine, sine_val, kv_heads, head_dim)
-    q_group = (
-        q_rot.reshape(tok_rows, kv_heads, group_size, head_dim)
-        .transpose(1, 2, 0, 3)
-        .reshape(kv_heads, group_size * tok_rows, head_dim)
-    )
-    score_scale = 1.0 / math.sqrt(head_dim)
-    softmax_state = (
-        jnp.full((kv_heads, group_size * tok_rows), NEG_FILL, jnp.float32),
-        jnp.zeros((kv_heads, group_size * tok_rows), jnp.float32),
-        jnp.zeros((kv_heads, group_size * tok_rows, head_dim), jnp.float32),
-    )
-    kv_pair = jnp.stack([k_rot, values])
-    softmax_state = online_update(
-        softmax_state, q_group, k_rot, values, query_pos, query_pos, query_start, score_scale
-    )
-
-    def cycle_free_step(turn_index, loop_state):
-        inner_state, moving = loop_state
-        moving = from_behind(moving, ("dp", "ctx"), 1)
-        source = my_block - turn_index - 1
-        inner_state = online_update(
-            inner_state,
-            q_group,
-            moving[0],
-            moving[1],
-            source * tok_rows + local_index,
-            query_pos,
-            query_start,
-            score_scale,
-        )
-        return (inner_state, moving)
-
-    softmax_state, _ = lax.fori_loop(0, reach_devs, cycle_free_step, (softmax_state, kv_pair))
-    row_max, row_sum, weighted = softmax_state
-    heads_out = (weighted / row_sum[..., None]).reshape(kv_heads, group_size, tok_rows, head_dim)
-    heads_out = (
-        heads_out.transpose(2, 0, 1, 3).reshape(tok_rows, num_heads * head_dim).astype(jnp.bfloat16)
-    )
+    heads_out = attention_phase(q_rot, k_rot, values, query_start)
     spread = lax.all_to_all(heads_out, "dp", split_axis=1, concat_axis=0, tiled=True)
     projected = lax.psum_scatter(
         jnp.dot(spread, w_out, preferred_element_type=jnp.float32).astype(jnp.bfloat16),

time: 503 us -> 338 us (0.67)
  starting transfers between devices: 99.8 us -> 0.01 us
  matrix products: 25.2 us -> 5.57 us
  blocking collectives: 90 us -> 72.5 us
  waiting for transfers between devices: 124 us -> 112 us
  local copies, waits for them, and re-layouts: 13.1 us -> 4.91 us
  other arithmetic: 12.8 us -> 7.03 us
    ppermute x16 -> x0, starting transfers between devices: 99.8 us -> none  [from_behind(): return lax.ppermute(block, axis, route)]
    dot_general x34 -> x0, matrix products: 18 us -> none  [the longest x17 12.2 us: online_update(): jnp.einsum('aqk,akd->aqd', weights.astype(jnp.bfloat16), value_heads, pre...]
    all_to_all x1, blocking collectives: 90 us -> 72.5 us  [per_device(): lax.all_to_all(heads_out, 'dp', split_axis=1, concat_axis=0, tiled=True)]
    ppermute x16 -> x0, waiting for transfers between devices: 14.3 us -> none  [from_behind(): return lax.ppermute(block, axis, route)]
  transfers between devices with their start and end apart: 17 -> 1, of which waited for: 17 -> 1; matrix products, arithmetic and copies ran while one was open for 1% -> 0% of each run, Pallas kernels for 0% -> 0%
where the time goes in v2:
time: 338 us; the launch traced here: 337 us
  Pallas kernels  121 us (36%)
  waiting for transfers between devices  112 us (33%)
  blocking collectives  72.5 us (21%)
  between operations  13.5 us (4%)
  other arithmetic  7.03 us (2%)
  matrix products  5.57 us (2%)
  local copies, waits for them, and re-layouts  4.91 us (1%)
    pallas_call x1, Pallas kernels, mlp_phase(): pl.pallas_call(mlp_kernel, out_shape=jax.ShapeDtypeStruct((rows, width),...  119 us
    reduce_scatter x1, waiting for transfers between devices, per_device(): lax.psum_scatter(jnp.dot(spread, w_out, preferred_element_type=jnp.float3...  112 us
    all_to_all x1, blocking collectives, per_device(): lax.all_to_all(heads_out, 'dp', split_axis=1, concat_axis=0, tiled=True)  72.5 us
  transfers between devices with their start and end apart: 1, of which 1 were waited for; matrix products, arithmetic and copies ran while one was open for 0% of the time, Pallas kernels for 0%

profile of v2, /device:TPU:0, one launch (start us, length us, event | category | flops | bytes accessed | tf_op | source)
XLA Modules:
  0.0 337.3 jit_solution(6243450829378738754)
XLA Ops:
  6.6 0.8 copy.14
  7.4 0.1 reduce
  7.5 0.7 sub.16
  8.2 0.1 select_reduce_fusion
  8.3 1.0 reshape.127
  9.3 0.3 multiply_cosine_fusion
  9.6 0.3 subtract_convert_fusion.1
  9.9 0.2 pad_maximum_fusion.1
  10.1 0.1 convert_bitcast_fusion
  10.2 0.2 copy.17
  10.4 0.5 subtract_convert_fusion
  11.0 0.3 pad_maximum_fusion
  11.3 0.1 copy.23
  11.4 0.1 broadcast_in_dim.13.start_ref
  11.5 0.4 copy-done
  11.9 1.9 attention_chain.1
  13.8 72.5 %all_to_all.19 = bf16[128,8,256]{2,0,1:T(8,128)(2,1)S(1)} all-to-all(bf16[128,8,256]{2,0,1:T(8,128)(2,1)S(1)} %bitcast.26), channel_id=1, replica_groups=mesh['dp'=8,'ctx'=16] {'dp'}, dimensions={1} | all-to-all | bytes 1048576 | tf_op jit(solution)/shard_map/all_to_all | solution.py:453
  86.3 5.6 %convolution_convert_fusion = bf16[1024,4096]{1,0:T(8,128)(2,1)} fusion(bf16[1024,256]{1,0:T(8,128)(2,1)S(1)} %bitcast.27, bf16[256,4096]{1,0:T(8,128)(2,1)S(1)} %copy-done.3), kind=kOutput, calls=%fused_computation | convolution fusion | flops 2151677952 | bytes 11010048 | tf_op jit(solution)/shard_map/dot_general | solution.py:455
  91.9 0.0 reduce-scatter.2.cloned.1.call-update
  92.0 112.5 %reduce-scatter.2.cloned.1.call-done = bf16[128,4096]{1,0:T(8,128)(2,1)} async-done(((bf16[1024,4096]{1,0:T(8,128)(2,1)}), bf16[128,4096]{1,0:T(8,128)(2,1)}) %reduce-scatter.2.cloned.1.call-update) | async-done | bytes 1048592 | tf_op jit(solution)/shard_map/reduce_scatter | solution.py:454
  204.4 3.0 convert_add_fusion
  207.5 1.4 multiply_convert_fusion.normed_ref
  208.8 119.3 %mlp_exchange.1 = bf16[128,4096]{1,0:T(8,128)(2,1)} custom-call(bf16[128,4096]{1,0:T(8,128)(2,1)} %multiply_convert_fusion.normed_ref, f32[128,4096]{1,0:T(8,128)} %get-tuple-element.5.resid_ref, bf16[4096,896]{1,0:T(8,128)(2,1)} %gate_hbm.1, bf16[4096,896]{1,0:T(8,128)(2,1)} %up_hbm.1, bf16[896,4096]{1,0:T(8,128)(2,1)} %down_hbm.1), custom_call_target="tpu_custom_call" | custom-call | tf_op jit(solution)/shard_map/mlp_exchange/pallas_call | solution.py:289
  328.1 2.3 copy.27
  (19 shorter events, 0.2 us)
Async XLA Ops:
  6.5 3.6 %copy-start.4 = (bf16[128,2048]{1,0:T(8,128)(2,1)S(1)}, bf16[128,2048]{1,0:T(8,128)(2,1)}, u32[]{:S(2)}) copy-start(bf16[128,2048]{1,0:T(8,128)(2,1)} %param.11) | copy-start | bytes 1572868
  6.5 197.9 %reduce-scatter.2.cloned.1.call-start = ((), (), s32[]{:S(2)}) async-start(), calls=%async_computation.2 | async-start | bytes 9437184 | tf_op jit(solution)/shard_map/reduce_scatter | solution.py:454
  11.0 0.9 copy-start
  11.3 75.1 %copy-start.3 = (bf16[256,4096]{1,0:T(8,128)(2,1)S(1)}, bf16[256,4096]{1,0:T(8,128)(2,1)}, u32[]{:S(2)}) copy-start(bf16[256,4096]{1,0:T(8,128)(2,1)} %param.15) | copy-start | bytes 6291460
  91.9 112.5 %copy-start.1 = (bf16[128,4096]{1,0:T(8,128)(2,1)S(1)}, bf16[128,4096]{1,0:T(8,128)(2,1)}, u32[]{:S(2)}) copy-start(bf16[128,4096]{1,0:T(8,128)(2,1)} %param.10) | copy-start | bytes 3145732
  91.9 115.5 %copy-start.5 = (f32[4096]{0:T(1024)S(1)}, f32[4096]{0:T(1024)}, u32[]{:S(2)}) copy-start(f32[4096]{0:T(1024)} %param.16) | copy-start | bytes 49156
  204.4 3.0 copy-start.2
Sparse Core Ops, SparseCore 0:
  92.1 112.3 reduce-scatter.1

commit v3 on v2

--- a/solution.py
+++ b/solution.py
@@ -451,12 +451,9 @@
     k_rot = rotate(keys, cosine, sine_val, kv_heads, head_dim)
     heads_out = attention_phase(q_rot, k_rot, values, query_start)
     spread = lax.all_to_all(heads_out, "dp", split_axis=1, concat_axis=0, tiled=True)
-    projected = lax.psum_scatter(
-        jnp.dot(spread, w_out, preferred_element_type=jnp.float32).astype(jnp.bfloat16),
-        "dp",
-        scatter_dimension=0,
-        tiled=True,
-    ).astype(jnp.float32)
+    partial = jnp.dot(spread, w_out, preferred_element_type=jnp.float32).astype(jnp.bfloat16)
+    parts = lax.all_to_all(partial, "dp", split_axis=0, concat_axis=0, tiled=True)
+    projected = jnp.sum(parts.reshape(-1, tok_rows, parts.shape[1]).astype(jnp.float32), axis=0)
     residual_sum = resid.astype(jnp.float32) + projected
     mean_sq = jnp.mean(residual_sum * residual_sum, axis=1, keepdims=True)
     normed = (residual_sum * lax.rsqrt(mean_sq + EPS) * norm_gain).astype(jnp.bfloat16)

time: 338 us -> 302 us (0.89)
  waiting for transfers between devices: 112 us -> 0 us
  blocking collectives: 72.5 us -> 169 us
  between operations: 13.5 us -> 0.18 us
    reduce_scatter x1 -> x0, waiting for transfers between devices: 112 us -> none  [per_device(): lax.psum_scatter(jnp.dot(spread, w_out, preferred_element_type=jnp.float3...]
    all_to_all x0 -> x1, blocking collectives: none -> 96.3 us  [per_device(): lax.all_to_all(partial, 'dp', split_axis=0, concat_axis=0, tiled=True)]
  transfers between devices with their start and end apart: 1 -> 0, of which waited for: 1 -> 0; matrix products, arithmetic and copies ran while one was open for 0% -> 0% of each run, Pallas kernels for 0% -> 0%
where the time goes in v3:
time: 302 us
  blocking collectives  169 us (56%)
  Pallas kernels  119 us (39%)
  local copies, waits for them, and re-layouts  6.25 us (2%)
  other arithmetic  5.74 us (2%)
    pallas_call x1, Pallas kernels, mlp_phase(): pl.pallas_call(mlp_kernel, out_shape=jax.ShapeDtypeStruct((rows, width),...  117 us
    all_to_all x1, blocking collectives, per_device(): lax.all_to_all(partial, 'dp', split_axis=0, concat_axis=0, tiled=True)  96.3 us
    all_to_all x1, blocking collectives, per_device(): lax.all_to_all(heads_out, 'dp', split_axis=1, concat_axis=0, tiled=True)  72.5 us

profile of v3, /device:TPU:0, one launch (start us, length us, event | category | flops | bytes accessed | tf_op | source)
XLA Modules:
  0.0 302.1 jit_solution(4453888066062592703)
XLA Ops:
  0.0 0.8 copy.14
  0.8 0.1 reduce
  1.0 0.7 sub.16
  1.6 0.1 select_reduce_fusion
  1.7 1.0 reshape.131
  2.7 0.3 multiply_cosine_fusion
  3.0 0.3 subtract_convert_fusion.1
  3.3 0.2 pad_maximum_fusion.1
  3.6 0.1 convert_bitcast_fusion
  3.7 0.2 copy.17
  3.9 0.5 subtract_convert_fusion
  4.4 0.3 pad_maximum_fusion
  4.7 0.1 copy.23
  5.0 0.4 copy-done
  5.3 1.9 attention_chain.1
  7.3 72.5 %all_to_all.28 = bf16[128,8,256]{2,0,1:T(8,128)(2,1)S(1)} all-to-all(bf16[128,8,256]{2,0,1:T(8,128)(2,1)S(1)} %bitcast.28), channel_id=1, replica_groups=mesh['dp'=8,'ctx'=16] {'dp'}, dimensions={1} | all-to-all | bytes 1048576 | tf_op jit(solution)/shard_map/all_to_all | solution.py:453
  79.8 2.3 convolution_convert_fusion
  82.2 96.3 %all_to_all.29 = bf16[8,128,4096]{2,1,0:T(8,128)(2,1)S(1)} all-to-all(bf16[8,128,4096]{2,1,0:T(8,128)(2,1)S(1)} %bitcast.25), channel_id=1, replica_groups=mesh['dp'=8,'ctx'=16] {'dp'}, dimensions={0} | all-to-all | bytes 16777216 | tf_op jit(solution)/shard_map/all_to_all | solution.py:455
  178.4 1.5 convert_reduce_fusion
  179.9 0.4 multiply_reduce_fusion
  180.3 1.3 copy-done.1
  181.7 1.2 multiply_convert_fusion.normed_ref
  182.9 116.9 %mlp_exchange.1 = bf16[128,4096]{1,0:T(8,128)(2,1)} custom-call(bf16[128,4096]{1,0:T(8,128)(2,1)} %multiply_convert_fusion.normed_ref, f32[128,4096]{1,0:T(8,128)} %copy-done.1, bf16[4096,896]{1,0:T(8,128)(2,1)} %gate_hbm.1, bf16[4096,896]{1,0:T(8,128)(2,1)} %up_hbm.1, bf16[896,4096]{1,0:T(8,128)(2,1)} %down_hbm.1), custom_call_target="tpu_custom_call" | custom-call | tf_op jit(solution)/shard_map/mlp_exchange/pallas_call | solution.py:289
  299.8 2.3 copy.27
  (18 shorter events, 0.2 us)
Async XLA Ops:
  0.0 3.6 %copy-start.4 = (bf16[128,2048]{1,0:T(8,128)(2,1)S(1)}, bf16[128,2048]{1,0:T(8,128)(2,1)}, u32[]{:S(2)}) copy-start(bf16[128,2048]{1,0:T(8,128)(2,1)} %param.11) | copy-start | bytes 1572868
  4.4 0.9 copy-start
  4.7 75.1 %copy-start.2 = (bf16[256,4096]{1,0:T(8,128)(2,1)S(1)}, bf16[256,4096]{1,0:T(8,128)(2,1)}, u32[]{:S(2)}) copy-start(bf16[256,4096]{1,0:T(8,128)(2,1)} %param.15) | copy-start | bytes 6291460
  178.4 1.5 copy-start.3
  179.9 1.8 copy-start.5
  180.3 1.4 copy-start.1
